TPU v7x, 256 devices: a whole 4x4x8 slice. The times are simulated.
256 devices in a mesh: side: 2 (over x_hi), row: 32 (over y, z), col: 4 (over x_lo, core).
Axes of the slice: x: 4 (x_hi: 2, x_lo: 2; x = x_hi * 2 + x_lo), y: 4, z: 8, core: 2. Of those that a mesh axis runs over, the one named last changes fastest.
Arguments:
- old_vectors: bfloat16 [2, 32768, 16384], P('side', 'row', 'col'), may hold values from -6 to 6
- reflectors: bfloat16 [2, 2, 32768, 512], P('side', None, 'row', 'col'), may hold values from -0.0625 to 0.0625
- triangles: float32 [2, 2, 512, 512], P('side'), may hold values from -0.25 to 0.25
- pole_sq: float32 [32768], replicated, may hold values from 1 to 65536, as said below
- coupling: float32 [32768], replicated, may hold values from -1 to 1
- deflated: int32 [32768], replicated, may hold values 0 or 1
- pole_order: int32 [32768], replicated, may hold values from 0 to 32767, each once
- anchors: int32 [1024], replicated, may hold values from 0 to 32766, as said below
- root_fraction: float32 [1024], replicated, may hold values from 0.2 to 0.8
Outputs:
- vectors: bfloat16 [2, 1024, 32768], P('side', 'col', 'row')
Inputs may be any that keep to these rules, and one draw needn't show every extreme that they name: `pole_sq`: strictly increasing; successive entries differ by 0.5 or more. `anchors`: distinct entries.
All inputs are finite; a program needn't handle non-finite values.
Results may differ from a plain program's by a relative error of at most 0.014.
Values may be sent and summed in bfloat16 or wider, within the bound.
A program may use at most 128 MiB of HBM per device.

v0:
```python
import jax
import jax.numpy as jnp
from jax import lax
from jax.sharding import PartitionSpec as P


def secular_columns(col_sq, col_coupling, col_live, weight, anchor_sq, pole_gap, root_fraction):
    denom = col_sq[:, None] - anchor_sq[None, :] - root_fraction[None, :] * pole_gap[None, :]
    return (col_live * col_coupling * weight)[:, None] / denom


def per_device(
    old_vectors,
    reflectors,
    triangles,
    pole_sq,
    coupling,
    deflated,
    pole_order,
    anchors,
    root_fraction,
):
    side_index = lax.axis_index("side")
    row_index = lax.axis_index("row")
    col_index = lax.axis_index("col")
    half_rows = lax.axis_size("row") // 2
    col_count = lax.axis_size("col")
    old_block = old_vectors[0]
    col_width = old_block.shape[1]
    order_size = pole_sq.shape[0]
    triplets = anchors.shape[0]
    local_triplets = triplets // col_count
    first_column = row_index // half_rows * (order_size // 2) + col_index * col_width
    columns = first_column + jnp.arange(col_width, dtype=jnp.int32)
    position = (
        jnp.zeros((order_size,), jnp.int32)
        .at[pole_order]
        .set(jnp.arange(order_size, dtype=jnp.int32))
    )
    sorted_pos = lax.dynamic_slice_in_dim(position, first_column, col_width)
    col_sq = pole_sq[sorted_pos]
    col_coupling = coupling[sorted_pos]
    col_live = (1 - deflated[sorted_pos]).astype(jnp.float32)
    weight = jnp.where(side_index == 0, jnp.ones_like(col_sq), jnp.sqrt(col_sq))
    anchor_sq = pole_sq[anchors]
    pole_gap = pole_sq[anchors + 1] - anchor_sq
    dead_triplet = deflated[anchors] == 1
    target = pole_order[anchors]
    secular = secular_columns(
        col_sq, col_coupling, col_live, weight, anchor_sq, pole_gap, root_fraction
    )
    onehot = (columns[:, None] == target[None, :]).astype(jnp.float32)
    mixing = jnp.where(dead_triplet[None, :], onehot, secular).astype(jnp.bfloat16)
    share_size = col_width // half_rows
    slice_part = lax.dynamic_slice_in_dim(
        secular, row_index % half_rows * share_size, share_size, 0
    )
    squares = lax.psum(jnp.sum(slice_part * slice_part, axis=0), ("row", "col"))
    col_scale = jnp.where(dead_triplet, jnp.ones_like(squares), 1.0 / jnp.sqrt(squares + 1e-06))
    merged = lax.psum_scatter(
        jnp.einsum("ck,rc->kr", mixing, old_block, preferred_element_type=jnp.float32).astype(
            jnp.bfloat16
        ),
        "col",
        scatter_dimension=0,
        tiled=True,
    ).astype(jnp.float32)
    my_scale = lax.dynamic_slice_in_dim(col_scale, col_index * local_triplets, local_triplets)
    vectors = merged * my_scale[:, None]
    panel_local = reflectors[0]
    panels = panel_local.shape[0]
    upper_tri = jnp.triu(triangles[0])
    highest = lax.Precision.HIGHEST
    for panel_index in reversed(range(panels)):
        panel_rows = panel_local[panel_index]
        current = vectors
        current_low = current.astype(jnp.bfloat16)
        projected = jnp.dot(
            current_low,
            lax.all_gather(panel_rows, "col", axis=1, tiled=True),
            preferred_element_type=jnp.float32,
        )
        projected = lax.psum(projected.astype(jnp.bfloat16), "row").astype(jnp.float32)
        coefficients = jnp.dot(projected, upper_tri[panel_index].T, precision=highest).astype(
            jnp.bfloat16
        )
        vectors = current - jnp.dot(
            coefficients,
            lax.all_gather(panel_rows, "col", axis=1, tiled=True).T,
            preferred_element_type=jnp.float32,
        )
    return vectors.astype(jnp.bfloat16)[None]


def solution(mesh):
    in_specs = (
        P("side", "row", "col"),
        P("side", None, "row", "col"),
        P("side", None, None, None),
        P(),
        P(),
        P(),
        P(),
        P(),
        P(),
    )
    out_specs = P("side", "col", "row")
    return jax.shard_map(
        per_device, mesh=mesh, in_specs=in_specs, out_specs=out_specs, check_vma=False
    )
```

profile of v0, /device:TPU:2, one launch (start us, length us, event | category | flops | bytes accessed | tf_op | source)
XLA Modules:
  0.0 883.1 jit_solution(16158088718118967877)
XLA Ops:
  6.5 1.9 fusion.23
  8.4 0.0 reduce-scatter.2.cloned.1.call-start
  8.5 0.9 compare_select_fusion
  9.5 120.1 %scatter_custom_fusion = s32[32768]{0:T(1024)S(1)} fusion(s32[32768]{0:T(1024)S(1)} %compare_select_fusion, s32[32768]{0:T(1024)S(1)} %iota.24, s32[]{:T(128)} %constant.23.clone.1), kind=kCustom, calls=%fused_computation.38 | custom fusion | bytes 131076 | tf_op jit(solution)/shard_map/scatter | solution.py:38
  129.6 19.5 %gather_fusion.2 = s32[4096]{0:T(1024)S(1)} fusion(s32[32768]{0:T(1024)} %param.14, s32[4096]{0:T(1024)S(1)} %fusion.20), kind=kCustom, calls=%fused_computation.2 | custom fusion | bytes 49152 | tf_op jit(solution)/shard_map/gather | solution.py:43
  149.2 23.0 %gather_fusion.4 = f32[4096]{0:T(1024)S(1)} fusion(f32[32768]{0:T(1024)S(1)} %copy-done, s32[4096]{0:T(1024)S(1)} %fusion.20), kind=kCustom, calls=%fused_computation.4 | custom fusion | bytes 49152 | tf_op jit(solution)/shard_map/gather | solution.py:41
  172.3 6.2 gather_fusion.5
  178.4 6.2 gather_fusion
  184.6 6.2 gather_fusion.1
  190.8 23.0 %gather_fusion.3 = f32[4096]{0:T(1024)S(1)} fusion(f32[32768]{0:T(1024)S(1)} %copy-done.2, s32[4096]{0:T(1024)S(1)} %fusion.20), kind=kCustom, calls=%fused_computation.3 | custom fusion | bytes 49152 | tf_op jit(solution)/shard_map/gather | solution.py:42
  213.8 6.2 gather_fusion.6
  220.0 6.5 subtract_divide_fusion
  226.5 1.3 multiply_reduce_fusion
  227.8 278.5 %psum.21 = f32[1024]{0:T(1024)S(1)} all-reduce(f32[1024]{0:T(1024)S(1)} %multiply_reduce_fusion), channel_id=1, replica_groups=mesh['side'=2,'row'=32,'col'=4] {'row','col'}, use_global_device_ids=true, to_apply=%region_3.4 | all-reduce | flops 1024 | bytes 8192 | tf_op jit(solution)/shard_map/psum | solution.py:58
  506.3 15.3 %fusion.5 = bf16[1024,1024]{1,0:T(8,128)(2,1)} fusion(bf16[1,1024,4096]{2,1,0:T(8,128)(2,1)} %param.9, s32[1024]{0:T(1024)S(1)} %gather_fusion.1, s32[4096]{0:T(1024)S(1)} %iota_add_fusion, pred[1024]{0:T(1024)(128)(4,1)S(1)} %get-tuple-element.6, f32[1024]{0:T(1024)S(1)} %subtract_multiply_fusion, f32[1024]{0:T(1024)S(1)} %gather_fusion.5, ...), kind=kOutput, calls=%fused_computation.16 | convolution fusion | flops 8620343296 | bytes 10548224 | tf_op jit(solution)/shard_map/ck,rc->kr/dot_general | solution.py:61
  521.7 0.0 all-reduce.3.cloned.1.call-start
  521.8 0.1 dynamic_slice.11
  521.8 28.4 %reduce-scatter.2.cloned.1.call-done = bf16[256,1024]{1,0:T(8,128)(2,1)} async-done(((bf16[1024,1024]{1,0:T(8,128)(2,1)}), bf16[256,1024]{1,0:T(8,128)(2,1)}) %reduce-scatter.2.cloned.1.call-update) | async-done | bytes 524304 | tf_op jit(solution)/shard_map/reduce_scatter | solution.py:60
  550.3 2.6 convolution_convert_fusion.3
  552.9 0.0 all-gather.7.cloned.1.call-start
  552.9 0.5 all-gather.7.cloned.1.call-update
  553.5 0.3 all-reduce.5.cloned.1.call-start
  553.7 0.2 iota_compare_fusion
  554.0 2.0 bitcast_select_fusion
  555.9 145.1 %all-reduce.3.cloned.1.call-done = bf16[256,512]{1,0:T(8,128)(2,1)} async-done(((bf16[256,512]{1,0:T(8,128)(2,1)}), bf16[256,512]{1,0:T(8,128)(2,1)}) %all-reduce.3.cloned.1.call-update) | async-done | bytes 262160 | tf_op jit(solution)/shard_map/psum | solution.py:83
  701.0 1.6 convolution_convert_fusion.2
  702.6 1.8 convolution_subtract_fusion.1
  704.5 18.7 %all-gather.7.cloned.1.call-done = bf16[1,1,1024,512]{3,2,1,0:T(8,128)(2,1)} async-done(((bf16[1,1,1024,128]{3,2,1,0:T(8,128)(2,1)}), bf16[1,1,1024,512]{3,2,1,0:T(8,128)(2,1)}) %all-gather.7.cloned.1.call-update) | async-done | bytes 1048592 | tf_op jit(solution)/shard_map/all_gather | solution.py:80
  723.1 2.4 convolution_convert_fusion.1
  725.5 146.9 %all-reduce.5.cloned.1.call-done = bf16[256,512]{1,0:T(8,128)(2,1)} async-done(((bf16[256,512]{1,0:T(8,128)(2,1)}), bf16[256,512]{1,0:T(8,128)(2,1)}) %all-reduce.5.cloned.1.call-update) | async-done | bytes 262160 | tf_op jit(solution)/shard_map/psum | solution.py:83
  872.4 1.6 convolution_convert_fusion
  874.1 2.5 fusion.9
  (26 shorter events, 0.2 us)
Async XLA Ops:
  6.5 142.6 %copy-start = (f32[32768]{0:T(1024)S(1)}, f32[32768]{0:T(1024)}, u32[]{:S(2)}) copy-start(f32[32768]{0:T(1024)} %param.12) | copy-start | bytes 393220
  6.5 515.3 %all-gather.5.cloned.1.call-start = ((), (), s32[]{:S(2)}) async-start(), calls=%async_computation.4 | async-start | bytes 1310720 | tf_op jit(solution)/shard_map/all_gather | solution.py:80
  8.4 541.8 %reduce-scatter.2.cloned.1.call-start = ((), (), s32[]{:S(2)}) async-start(), calls=%async_computation.1 | async-start | bytes 2621440 | tf_op jit(solution)/shard_map/reduce_scatter | solution.py:60
  129.6 42.6 %copy-start.4 = (s32[1024]{0:T(1024)S(1)}, s32[1024]{0:T(1024)}, u32[]{:S(2)}) copy-start(s32[1024]{0:T(1024)} %param.16) | copy-start | bytes 12292
  129.6 48.8 %copy-start.1 = (s32[32768]{0:T(1024)S(1)}, s32[32768]{0:T(1024)}, u32[]{:S(2)}) copy-start(s32[32768]{0:T(1024)} %param.14) | copy-start | bytes 393220
  149.2 35.4 %copy-start.3 = (s32[32768]{0:T(1024)S(1)}, s32[32768]{0:T(1024)}, u32[]{:S(2)}) copy-start(s32[32768]{0:T(1024)} %param.15) | copy-start | bytes 393220
  149.2 41.6 %copy-start.2 = (f32[32768]{0:T(1024)S(1)}, f32[32768]{0:T(1024)}, u32[]{:S(2)}) copy-start(f32[32768]{0:T(1024)} %param.13) | copy-start | bytes 393220
  172.3 47.7 %copy-start.5 = (f32[1024]{0:T(1024)S(1)}, f32[1024]{0:T(1024)}, u32[]{:S(2)}) copy-start(f32[1024]{0:T(1024)} %param.17) | copy-start | bytes 12292
  521.7 179.3 %all-reduce.3.cloned.1.call-start = ((), (), s32[]{:S(2)}) async-start(), calls=%async_computation.2 | async-start | bytes 524288 | tf_op jit(solution)/shard_map/psum | solution.py:83
  552.9 170.3 %all-gather.7.cloned.1.call-start = ((), (), s32[]{:S(2)}) async-start(), calls=%async_computation.5 | async-start | bytes 1310720 | tf_op jit(solution)/shard_map/all_gather | solution.py:80
  553.5 319.0 %all-reduce.5.cloned.1.call-start = ((), (), s32[]{:S(2)}) async-start(), calls=%async_computation.3 | async-start | bytes 524288 | tf_op jit(solution)/shard_map/psum | solution.py:83
Sparse Core Ops, SparseCore 0:
  9.2 26.2 all-gather.4
  521.8 28.4 reduce-scatter.1
  554.1 146.8 all-reduce.2
  702.8 20.2 all-gather.6
  726.8 145.5 all-reduce.4
where the time goes:
time: 884 us; the launch traced here: 883 us
  waiting for transfers between devices  340 us (38%)
  blocking collectives  278 us (31%)
  local copies, waits for them, and re-layouts  212 us (24%)
  matrix products  27.8 us (3%)
  between operations  13.4 us (2%)
  other arithmetic  10.9 us (1%)
    psum x2, waiting for transfers between devices, per_device(): lax.psum(projected.astype(jnp.bfloat16), 'row').astype(jnp.float32)  292 us
    psum x1, blocking collectives, per_device(): squares = lax.psum(jnp.sum(slice_part * slice_part, axis=0), ('row', 'col'))  278 us
    scatter x1, local copies, waits for them, and re-layouts, per_device(): position = jnp.zeros((order_size,), jnp.int32).at[pole_order].set(jnp.ara...  120 us
    reduce_scatter x1, waiting for transfers between devices, per_device(): lax.psum_scatter(jnp.einsum('ck,rc->kr', mixing, old_block, preferred_ele...  28.4 us
    gather x1, local copies, waits for them, and re-layouts, per_device(): col_sq = pole_sq[sorted_pos]  23 us
    gather x1, local copies, waits for them, and re-layouts, per_device(): col_coupling = coupling[sorted_pos]  23 us
    gather x1, local copies, waits for them, and re-layouts, per_device(): col_live = (1 - deflated[sorted_pos]).astype(jnp.float32)  19.5 us
    all_gather x2, waiting for transfers between devices, per_device(): lax.all_gather(panel_rows, 'col', axis=1, tiled=True)  18.7 us
  transfers between devices with their start and end apart: 5, of which 4 were waited for; matrix products, arithmetic and copies ran while one was open for 27% of the time, Pallas kernels for 0%

commit v1 on v0

--- a/solution.py
+++ b/solution.py
@@ -55,7 +55,9 @@
     slice_part = lax.dynamic_slice_in_dim(
         secular, row_index % half_rows * share_size, share_size, 0
     )
-    squares = lax.psum(jnp.sum(slice_part * slice_part, axis=0), ("row", "col"))
+    work_x = jnp.sum(slice_part * slice_part, axis=0)
+    v_next = jax.lax.psum(work_x, "col")
+    squares = jax.lax.psum(v_next, "row")
     col_scale = jnp.where(dead_triplet, jnp.ones_like(squares), 1.0 / jnp.sqrt(squares + 1e-06))
     merged = lax.psum_scatter(
         jnp.einsum("ck,rc->kr", mixing, old_block, preferred_element_type=jnp.float32).astype(

time: 884 us -> 684 us (0.77)
  blocking collectives: 278 us -> 84 us
    psum x1 -> x2, blocking collectives: 278 us -> 84 us  [the longest x1 78.2 us: per_device(): squares = jax.lax.psum(v_next, 'row')]
  transfers between devices with their start and end apart: 5 -> 5, of which waited for: 4 -> 4; matrix products, arithmetic and copies ran while one was open for 27% -> 35% of each run, Pallas kernels for 0% -> 0%
where the time goes in v1:
time: 684 us
  waiting for transfers between devices  335 us (49%)
  local copies, waits for them, and re-layouts  212 us (31%)
  blocking collectives  84 us (12%)
  matrix products  27.8 us (4%)
  between operations  13.4 us (2%)
  other arithmetic  10.9 us (2%)
    psum x2, waiting for transfers between devices, per_device(): lax.psum(projected.astype(jnp.bfloat16), 'row').astype(jnp.float32)  292 us
    scatter x1, local copies, waits for them, and re-layouts, per_device(): position = jnp.zeros((order_size,), jnp.int32).at[pole_order].set(jnp.ara...  120 us
    psum x1, blocking collectives, per_device(): squares = jax.lax.psum(v_next, 'row')  78.2 us
    reduce_scatter x1, waiting for transfers between devices, per_device(): lax.psum_scatter(jnp.einsum('ck,rc->kr', mixing, old_block, preferred_ele...  23.5 us
    gather x1, local copies, waits for them, and re-layouts, per_device(): col_sq = pole_sq[sorted_pos]  23 us
    gather x1, local copies, waits for them, and re-layouts, per_device(): col_coupling = coupling[sorted_pos]  23 us
    gather x1, local copies, waits for them, and re-layouts, per_device(): col_live = (1 - deflated[sorted_pos]).astype(jnp.float32)  19.5 us
    all_gather x2, waiting for transfers between devices, per_device(): lax.all_gather(panel_rows, 'col', axis=1, tiled=True)  18.7 us
  transfers between devices with their start and end apart: 5, of which 4 were waited for; matrix products, arithmetic and copies ran while one was open for 35% of the time, Pallas kernels for 0%

profile of v1, /device:TPU:2, one launch (start us, length us, event | category | flops | bytes accessed | tf_op | source)
XLA Modules:
  0.0 683.6 jit_solution(9595648558337570840)
XLA Ops:
  6.5 1.9 fusion.23
  8.4 0.0 reduce-scatter.2.cloned.1.call-start
  8.5 0.9 compare_select_fusion
  9.5 120.1 %scatter_custom_fusion = s32[32768]{0:T(1024)S(1)} fusion(s32[32768]{0:T(1024)S(1)} %compare_select_fusion, s32[32768]{0:T(1024)S(1)} %iota.24, s32[]{:T(128)} %constant.23.clone.1), kind=kCustom, calls=%fused_computation.38 | custom fusion | bytes 131076 | tf_op jit(solution)/shard_map/scatter | solution.py:38
  129.6 19.5 %gather_fusion.2 = s32[4096]{0:T(1024)S(1)} fusion(s32[32768]{0:T(1024)} %param.14, s32[4096]{0:T(1024)S(1)} %fusion.20), kind=kCustom, calls=%fused_computation.2 | custom fusion | bytes 49152 | tf_op jit(solution)/shard_map/gather | solution.py:43
  149.2 23.0 %gather_fusion.4 = f32[4096]{0:T(1024)S(1)} fusion(f32[32768]{0:T(1024)S(1)} %copy-done, s32[4096]{0:T(1024)S(1)} %fusion.20), kind=kCustom, calls=%fused_computation.4 | custom fusion | bytes 49152 | tf_op jit(solution)/shard_map/gather | solution.py:41
  172.3 6.2 gather_fusion.5
  178.4 6.2 gather_fusion
  184.6 6.2 gather_fusion.1
  190.8 23.0 %gather_fusion.3 = f32[4096]{0:T(1024)S(1)} fusion(f32[32768]{0:T(1024)S(1)} %copy-done.2, s32[4096]{0:T(1024)S(1)} %fusion.20), kind=kCustom, calls=%fused_computation.3 | custom fusion | bytes 49152 | tf_op jit(solution)/shard_map/gather | solution.py:42
  213.8 6.2 gather_fusion.6
  220.0 6.4 subtract_divide_fusion
  226.5 1.3 multiply_reduce_fusion
  227.8 5.8 psum.28
  233.6 78.2 %psum.29 = f32[1024]{0:T(1024)S(1)} all-reduce(f32[1024]{0:T(1024)S(1)} %psum.28), channel_id=1, replica_groups=mesh['side'=2,'row'=32,'col'=4] {'row'}, use_global_device_ids=true, to_apply=%region_4.5 | all-reduce | flops 1024 | bytes 8192 | tf_op jit(solution)/shard_map/psum | solution.py:60
  311.8 15.3 %fusion.5 = bf16[1024,1024]{1,0:T(8,128)(2,1)} fusion(bf16[1,1024,4096]{2,1,0:T(8,128)(2,1)} %param.9, s32[1024]{0:T(1024)S(1)} %gather_fusion.1, s32[4096]{0:T(1024)S(1)} %iota_add_fusion, pred[1024]{0:T(1024)(128)(4,1)S(1)} %get-tuple-element.6, f32[1024]{0:T(1024)S(1)} %subtract_multiply_fusion, f32[1024]{0:T(1024)S(1)} %gather_fusion.5, ...), kind=kOutput, calls=%fused_computation.16 | convolution fusion | flops 8620343296 | bytes 10548224 | tf_op jit(solution)/shard_map/ck,rc->kr/dot_general | solution.py:63
  327.2 0.0 all-reduce.3.cloned.1.call-start
  327.2 0.1 dynamic_slice.11
  327.3 23.5 %reduce-scatter.2.cloned.1.call-done = bf16[256,1024]{1,0:T(8,128)(2,1)} async-done(((bf16[1024,1024]{1,0:T(8,128)(2,1)}), bf16[256,1024]{1,0:T(8,128)(2,1)}) %reduce-scatter.2.cloned.1.call-update) | async-done | bytes 524304 | tf_op jit(solution)/shard_map/reduce_scatter | solution.py:62
  350.8 2.6 convolution_convert_fusion.3
  353.5 0.5 all-gather.7.cloned.1.call-update
  354.0 0.3 all-reduce.5.cloned.1.call-start
  354.3 0.2 iota_compare_fusion
  354.5 2.0 bitcast_select_fusion
  356.4 145.1 %all-reduce.3.cloned.1.call-done = bf16[256,512]{1,0:T(8,128)(2,1)} async-done(((bf16[256,512]{1,0:T(8,128)(2,1)}), bf16[256,512]{1,0:T(8,128)(2,1)}) %all-reduce.3.cloned.1.call-update) | async-done | bytes 262160 | tf_op jit(solution)/shard_map/psum | solution.py:85
  501.6 1.6 convolution_convert_fusion.2
  503.2 1.8 convolution_subtract_fusion.1
  505.0 18.7 %all-gather.7.cloned.1.call-done = bf16[1,1,1024,512]{3,2,1,0:T(8,128)(2,1)} async-done(((bf16[1,1,1024,128]{3,2,1,0:T(8,128)(2,1)}), bf16[1,1,1024,512]{3,2,1,0:T(8,128)(2,1)}) %all-gather.7.cloned.1.call-update) | async-done | bytes 1048592 | tf_op jit(solution)/shard_map/all_gather | solution.py:82
  523.7 2.4 convolution_convert_fusion.1
  526.1 146.9 %all-reduce.5.cloned.1.call-done = bf16[256,512]{1,0:T(8,128)(2,1)} async-done(((bf16[256,512]{1,0:T(8,128)(2,1)}), bf16[256,512]{1,0:T(8,128)(2,1)}) %all-reduce.5.cloned.1.call-update) | async-done | bytes 262160 | tf_op jit(solution)/shard_map/psum | solution.py:85
  673.0 1.6 convolution_convert_fusion
  674.6 2.5 fusion.9
  (27 shorter events, 0.2 us)
Async XLA Ops:
  6.5 142.6 %copy-start = (f32[32768]{0:T(1024)S(1)}, f32[32768]{0:T(1024)}, u32[]{:S(2)}) copy-start(f32[32768]{0:T(1024)} %param.12) | copy-start | bytes 393220
  6.5 320.8 %all-gather.5.cloned.1.call-start = ((), (), s32[]{:S(2)}) async-start(), calls=%async_computation.4 | async-start | bytes 1310720 | tf_op jit(solution)/shard_map/all_gather | solution.py:82
  8.4 342.3 %reduce-scatter.2.cloned.1.call-start = ((), (), s32[]{:S(2)}) async-start(), calls=%async_computation.1 | async-start | bytes 2621440 | tf_op jit(solution)/shard_map/reduce_scatter | solution.py:62
  129.6 42.6 %copy-start.4 = (s32[1024]{0:T(1024)S(1)}, s32[1024]{0:T(1024)}, u32[]{:S(2)}) copy-start(s32[1024]{0:T(1024)} %param.16) | copy-start | bytes 12292
  129.6 48.8 %copy-start.1 = (s32[32768]{0:T(1024)S(1)}, s32[32768]{0:T(1024)}, u32[]{:S(2)}) copy-start(s32[32768]{0:T(1024)} %param.14) | copy-start | bytes 393220
  149.2 35.4 %copy-start.3 = (s32[32768]{0:T(1024)S(1)}, s32[32768]{0:T(1024)}, u32[]{:S(2)}) copy-start(s32[32768]{0:T(1024)} %param.15) | copy-start | bytes 393220
  149.2 41.6 %copy-start.2 = (f32[32768]{0:T(1024)S(1)}, f32[32768]{0:T(1024)}, u32[]{:S(2)}) copy-start(f32[32768]{0:T(1024)} %param.13) | copy-start | bytes 393220
  172.3 47.7 %copy-start.5 = (f32[1024]{0:T(1024)S(1)}, f32[1024]{0:T(1024)}, u32[]{:S(2)}) copy-start(f32[1024]{0:T(1024)} %param.17) | copy-start | bytes 12292
  327.2 174.4 %all-reduce.3.cloned.1.call-start = ((), (), s32[]{:S(2)}) async-start(), calls=%async_computation.2 | async-start | bytes 524288 | tf_op jit(solution)/shard_map/psum | solution.py:85
  353.4 170.3 %all-gather.7.cloned.1.call-start = ((), (), s32[]{:S(2)}) async-start(), calls=%async_computation.5 | async-start | bytes 1310720 | tf_op jit(solution)/shard_map/all_gather | solution.py:82
  354.0 319.0 %all-reduce.5.cloned.1.call-start = ((), (), s32[]{:S(2)}) async-start(), calls=%async_computation.3 | async-start | bytes 524288 | tf_op jit(solution)/shard_map/psum | solution.py:85
Sparse Core Ops, SparseCore 0:
  9.2 26.2 all-gather.4
  327.3 23.4 reduce-scatter.1
  354.7 146.8 all-reduce.2
  503.4 20.2 all-gather.6
  527.4 145.5 all-reduce.4
